TPU v7x, 32 devices: a whole 2x2x4 slice. The times are simulated.
32 devices in a mesh: grp: 2 (over y), row: 4 (over x, core), col: 4 (over z).
Axes of the slice: x: 2, y: 2, z: 4, core: 2. Of those that a mesh axis runs over, the one named last changes fastest.
Arguments:
- programs: bfloat16 [2048, 2048], P(('grp', 'row'), 'col'), parts along dimension 0, may hold values from -6 to 6
- tests: bfloat16 [2048, 2048], P(('grp', 'col'), 'row'), parts along dimension 0, may hold values from -6 to 6
- weight: bfloat16 [2048, 2048], P('col', 'row'), may hold values from -0.125 to 0.125
- labels: int32 [2048, 1024], P(('grp', 'row'), 'col'), parts along dimension 0, may hold values 0 or 1
Outputs:
- grad_programs: bfloat16 [2048, 2048], P(('grp', 'row'), 'col'), parts along dimension 0
- grad_tests: bfloat16 [2048, 2048], P(('grp', 'col'), 'row'), parts along dimension 0
- grad_weight: float32 [4096, 2048], P(('grp', 'col'), 'row'), parts along dimension 0
There are 2 independent parts, one for each index of `grp`. A program takes and returns all parts, laid end to end along the dimension named above; an argument that names none is the same for every part. Nothing has to cross between parts.
All inputs are finite; a program needn't handle non-finite values. No bound on the sum of `labels` on one device may be relied on, other than what follows from the above.
Results may differ from a plain program's by a relative error of at most 0.017.
Values may be sent and summed in bfloat16 or wider, within the bound.
A program may use at most 64 MiB of HBM per device.

v0:
```python
import math
import jax
import jax.numpy as jnp
from jax import lax
from jax.sharding import PartitionSpec as P

E = 2048


def contract(left, right, left_dim, right_dim):
    return lax.dot_general(
        left, right, (((left_dim,), (right_dim,)), ((), ())), preferred_element_type=jnp.float32
    )


def local(programs, tests, weight, labels):
    factor = 1.0 / math.sqrt(E)
    targets = labels.astype(jnp.float32)
    w_rows = lax.all_gather(weight, "row", axis=1, tiled=True)
    share = lax.psum_scatter(
        jnp.dot(programs, w_rows, preferred_element_type=jnp.float32).astype(jnp.bfloat16),
        "col",
        scatter_dimension=0,
        tiled=True,
    )
    projected = lax.all_gather(share, "col", axis=0, tiled=True)
    test_whole = lax.all_gather(tests, "row", axis=1, tiled=True)
    logits = contract(projected, test_whole, 1, 1) * factor
    dlogits = (jax.nn.sigmoid(logits) - targets).astype(jnp.bfloat16)
    partial_sums = jnp.dot(dlogits, test_whole, preferred_element_type=jnp.float32)
    summed = lax.psum(partial_sums.astype(jnp.bfloat16), "col")
    grad_programs = (contract(summed, w_rows, 1, 1) * factor).astype(jnp.bfloat16)
    weight_part = contract(programs, summed, 0, 0) * factor
    test_part = contract(dlogits, projected, 0, 0) * factor
    grad_weight, test_total = (
        lax.psum_scatter(
            weight_part.astype(jnp.bfloat16), "row", scatter_dimension=1, tiled=True
        ).astype(jnp.float32),
        lax.psum_scatter(
            test_part.astype(jnp.bfloat16), "row", scatter_dimension=1, tiled=True
        ).astype(jnp.float32),
    )
    grad_tests = test_total.astype(jnp.bfloat16)
    return (grad_programs, grad_tests, grad_weight)


def solution(mesh):
    placed = (
        P(("grp", "row"), "col"),
        P(("grp", "col"), "row"),
        P("col", "row"),
        P(("grp", "row"), "col"),
    )
    return jax.shard_map(
        local,
        mesh=mesh,
        in_specs=placed,
        out_specs=(P(("grp", "row"), "col"), P(("grp", "col"), "row"), P(("grp", "col"), "row")),
        check_vma=False,
    )
```

profile of v0, /device:TPU:0, one launch (start us, length us, event | category | flops | bytes accessed | tf_op | source)
XLA Modules:
  0.0 236.3 jit_solution(9814701826729110321)
XLA Ops:
  7.2 0.0 all-gather.4.cloned.1.call-start
  7.2 0.7 all-gather.4.cloned.1.call-update
  7.9 0.0 reduce-scatter.4.cloned.1.call-start
  8.0 26.9 %all-gather.4.cloned.1.call-done = bf16[512,2048]{1,0:T(8,128)(2,1)} async-done(((bf16[512,512]{1,0:T(8,128)(2,1)}), bf16[512,2048]{1,0:T(8,128)(2,1)}) %all-gather.4.cloned.1.call-update) | async-done | bytes 2097168 | tf_op jit(solution)/shard_map/all_gather | solution.py:19
  34.9 3.3 %convolution_convert_fusion = bf16[256,2048]{1,0:T(8,128)(2,1)} fusion(bf16[256,512]{1,0:T(8,128)(2,1)S(1)} %copy-done, bf16[512,2048]{1,0:T(8,128)(2,1)} %all-gather.4.cloned.1.call-done), kind=kOutput, calls=%fused_computation.3 | convolution fusion | flops 537395200 | bytes 3407872 | tf_op jit(solution)/shard_map/dot_general | solution.py:21
  38.2 0.0 all-gather.8.cloned.1.call-start
  38.2 0.7 all-gather.8.cloned.1.call-update
  38.9 0.0 all-gather.6.cloned.1.call-start
  39.0 26.5 %reduce-scatter.4.cloned.1.call-done = bf16[64,2048]{1,0:T(8,128)(2,1)} async-done(((bf16[256,2048]{1,0:T(8,128)(2,1)}), bf16[64,2048]{1,0:T(8,128)(2,1)}) %reduce-scatter.4.cloned.1.call-update) | async-done | bytes 262160 | tf_op jit(solution)/shard_map/reduce_scatter | solution.py:20
  65.5 0.0 all-reduce.2.cloned.1.call-start
  65.6 17.0 %all-gather.8.cloned.1.call-done = bf16[256,2048]{1,0:T(8,128)(2,1)} async-done(((bf16[256,512]{1,0:T(8,128)(2,1)}), bf16[256,2048]{1,0:T(8,128)(2,1)}) %all-gather.8.cloned.1.call-update) | async-done | bytes 1048592 | tf_op jit(solution)/shard_map/all_gather | solution.py:27
  82.6 29.5 %all-gather.6.cloned.1.call-done = bf16[256,2048]{1,0:T(8,128)(2,1)} async-done(((bf16[64,2048]{1,0:T(8,128)(2,1)}), bf16[256,2048]{1,0:T(8,128)(2,1)}) %all-gather.6.cloned.1.call-update) | async-done | bytes 1048592 | tf_op jit(solution)/shard_map/all_gather | solution.py:26
  112.0 2.0 fusion.8
  114.1 1.4 convolution_convert_fusion.1
  115.5 0.0 reduce-scatter.8.cloned.1.call-start
  115.6 51.4 %all-reduce.2.cloned.1.call-done = bf16[256,2048]{1,0:T(8,128)(2,1)} async-done(((bf16[256,2048]{1,0:T(8,128)(2,1)}), bf16[256,2048]{1,0:T(8,128)(2,1)}) %all-reduce.2.cloned.1.call-update) | async-done | bytes 1048592 | tf_op jit(solution)/shard_map/psum | solution.py:31
  167.0 3.3 %fusion = bf16[512,2048]{0,1:T(8,128)(2,1)} fusion(bf16[256,2048]{1,0:T(8,128)(2,1)} %all-reduce.2.cloned.1.call-done, bf16[256,512]{1,0:T(8,128)(2,1)S(1)} %copy-done), kind=kOutput, calls=%fused_computation.1 | convolution fusion | flops 538968064 | bytes 3407872 | tf_op jit(solution)/shard_map/dot_general | solution.py:11
  170.3 0.0 reduce-scatter.6.cloned.1.call-start
  170.4 1.1 copy-done.2
  171.5 1.4 fusion.1
  173.0 2.7 %fusion.2 = bf16[256,512]{1,0:T(8,128)(2,1)} fusion(bf16[256,2048]{1,0:T(8,128)(2,1)} %all-reduce.2.cloned.1.call-done, bf16[512,2048]{1,0:T(8,128)(2,1)S(1)} %copy-done.1), kind=kOutput, calls=%fused_computation.7 | convolution fusion | flops 537133056 | bytes 3407872 | tf_op jit(solution)/shard_map/dot_general | solution.py:11
  175.6 25.6 %reduce-scatter.8.cloned.1.call-done = bf16[512,512]{0,1:T(8,128)(2,1)} async-done(((bf16[512,2048]{0,1:T(8,128)(2,1)}), bf16[512,512]{0,1:T(8,128)(2,1)}) %reduce-scatter.8.cloned.1.call-update) | async-done | bytes 524304 | tf_op jit(solution)/shard_map/reduce_scatter | solution.py:36
  201.3 2.2 copy.7
  203.5 25.9 %reduce-scatter.6.cloned.1.call-done = bf16[256,512]{1,0:T(8,128)(2,1)} async-done(((bf16[256,2048]{1,0:T(8,128)(2,1)}), bf16[256,512]{1,0:T(8,128)(2,1)}) %reduce-scatter.6.cloned.1.call-update) | async-done | bytes 262160 | tf_op jit(solution)/shard_map/reduce_scatter | solution.py:39
  (14 shorter events, 0.1 us)
Async XLA Ops:
  7.2 27.7 %copy-start = (bf16[256,512]{1,0:T(8,128)(2,1)S(1)}, bf16[256,512]{1,0:T(8,128)(2,1)}, u32[]{:S(2)}) copy-start(bf16[256,512]{1,0:T(8,128)(2,1)} %param.4) | copy-start | bytes 786436
  7.2 27.7 %all-gather.4.cloned.1.call-start = ((), (), s32[]{:S(2)}) async-start(), calls=%async_computation.3 | async-start | bytes 2621440 | tf_op jit(solution)/shard_map/all_gather | solution.py:19
  7.9 104.1 %copy-start.4 = (s32[256,256]{1,0:T(8,128)S(1)}, s32[256,256]{1,0:T(8,128)}, u32[]{:S(2)}) copy-start(s32[256,256]{1,0:T(8,128)} %param.7) | copy-start | bytes 786436
  7.9 57.6 %reduce-scatter.4.cloned.1.call-start = ((), (), s32[]{:S(2)}) async-start(), calls=%async_computation.4 | async-start | bytes 1310720 | tf_op jit(solution)/shard_map/reduce_scatter | solution.py:20
  38.2 44.4 %all-gather.8.cloned.1.call-start = ((), (), s32[]{:S(2)}) async-start(), calls=%async_computation.6 | async-start | bytes 1310720 | tf_op jit(solution)/shard_map/all_gather | solution.py:27
  38.9 73.1 %all-gather.6.cloned.1.call-start = ((), (), s32[]{:S(2)}) async-start(), calls=%async_computation.5 | async-start | bytes 1310720 | tf_op jit(solution)/shard_map/all_gather | solution.py:26
  65.5 101.5 %all-reduce.2.cloned.1.call-start = ((), (), s32[]{:S(2)}) async-start(), calls=%async_computation.7 | async-start | bytes 2097152 | tf_op jit(solution)/shard_map/psum | solution.py:31
  82.5 31.5 %copy-start.3 = (bf16[256,2048]{1,0:T(8,128)(2,1)S(1)}, bf16[256,2048]{1,0:T(8,128)(2,1)}, u32[]{:S(2)}) copy-start(bf16[256,2048]{1,0:T(8,128)(2,1)} %all-gather.8.cloned.1.call-done) | copy-start | bytes 3145732
  115.5 85.7 %reduce-scatter.8.cloned.1.call-start = ((), (), s32[]{:S(2)}) async-start(), calls=%async_computation.9 | async-start | bytes 2621440 | tf_op jit(solution)/shard_map/reduce_scatter | solution.py:36
  170.3 1.2 copy-start.2
  170.3 2.7 %copy-start.1 = (bf16[512,2048]{1,0:T(8,128)(2,1)S(1)}, bf16[512,2048]{1,0:T(8,128)(2,1)}, u32[]{:S(2)}) copy-start(bf16[512,2048]{1,0:T(8,128)(2,1)} %all-gather.4.cloned.1.call-done) | copy-start | bytes 6291460
  170.3 59.1 %reduce-scatter.6.cloned.1.call-start = ((), (), s32[]{:S(2)}) async-start(), calls=%async_computation.8 | async-start | bytes 1310720 | tf_op jit(solution)/shard_map/reduce_scatter | solution.py:39
Sparse Core Ops, SparseCore 0:
  9.6 25.2 all-gather.3
  38.3 27.1 reduce-scatter.3
  67.1 15.3 all-gather.7
  84.1 27.9 all-gather.5
  115.6 51.3 all-reduce.1
  170.4 30.7 reduce-scatter.7
  204.5 24.8 reduce-scatter.5
where the time goes:
time: 237 us; the launch traced here: 236 us
  waiting for transfers between devices  204 us (86%)
  between operations  14.2 us (6%)
  matrix products  14.1 us (6%)
  local copies, waits for them, and re-layouts  3.38 us (1%)
    psum x1, waiting for transfers between devices, local(): summed = lax.psum(partial_sums.astype(jnp.bfloat16), 'col')  51.4 us
    all_gather x1, waiting for transfers between devices, local(): projected = lax.all_gather(share, 'col', axis=0, tiled=True)  29.5 us
    all_gather x1, waiting for transfers between devices, local(): w_rows = lax.all_gather(weight, 'row', axis=1, tiled=True)  26.9 us
    reduce_scatter x1, waiting for transfers between devices, local(): lax.psum_scatter(jnp.dot(programs, w_rows, preferred_element_type=jnp.flo...  26.5 us
    reduce_scatter x1, waiting for transfers between devices, local(): lax.psum_scatter(test_part.astype(jnp.bfloat16), 'row', scatter_dimension...  25.9 us
    reduce_scatter x1, waiting for transfers between devices, local(): lax.psum_scatter(weight_part.astype(jnp.bfloat16), 'row', scatter_dimensi...  25.6 us
    all_gather x1, waiting for transfers between devices, local(): test_whole = lax.all_gather(tests, 'row', axis=1, tiled=True)  17 us
    dot_general x4, matrix products, contract(): lax.dot_general(left, right, (((left_dim,), (right_dim,)), ((), ())), pre...  9.44 us
  transfers between devices with their start and end apart: 7, of which 7 were waited for; matrix products, arithmetic and copies ran while one was open for 3% of the time, Pallas kernels for 0%

commit v1 on v0

--- a/solution.py
+++ b/solution.py
@@ -23,7 +23,22 @@
         scatter_dimension=0,
         tiled=True,
     )
-    projected = lax.all_gather(share, "col", axis=0, tiled=True)
+    ways, here, step = (lax.axis_size("col"), lax.axis_index("col"), share.shape[0])
+    lengths = [n * ways if d == 0 else n for d, n in enumerate(share.shape)]
+    projected = lax.dynamic_update_slice_in_dim(
+        jnp.zeros(lengths, share.dtype), share, here * step, axis=0
+    )
+    going_up = going_down = share
+    for far in range(1, ways // 2 + 1):
+        going_up = lax.ppermute(going_up, "col", [(d, (d + 1) % ways) for d in range(ways)])
+        projected = lax.dynamic_update_slice_in_dim(
+            projected, going_up, (here - far) % ways * step, axis=0
+        )
+        if 2 * far < ways:
+            going_down = lax.ppermute(going_down, "col", [(d, (d - 1) % ways) for d in range(ways)])
+            projected = lax.dynamic_update_slice_in_dim(
+                projected, going_down, (here + far) % ways * step, axis=0
+            )
     test_whole = lax.all_gather(tests, "row", axis=1, tiled=True)
     logits = contract(projected, test_whole, 1, 1) * factor
     dlogits = (jax.nn.sigmoid(logits) - targets).astype(jnp.bfloat16)

time: 237 us -> 210 us (0.89)
  waiting for transfers between devices: 204 us -> 173 us
  starting transfers between devices: 0.28 us -> 4.07 us
    all_gather x1 -> x0, waiting for transfers between devices: 29.5 us -> none  [local(): projected = lax.all_gather(share, 'col', axis=0, tiled=True)]
    all_gather x1, waiting for transfers between devices: 17 us -> 0.02 us  [local(): test_whole = lax.all_gather(tests, 'row', axis=1, tiled=True)]
    ppermute x0 -> x3, waiting for transfers between devices: none -> 16.2 us  [the longest x2 13.7 us: local(): lax.ppermute(going_up, 'col', [(d, (d + 1) % ways) for d in range(ways)])]
    ppermute x0 -> x3, starting transfers between devices: none -> 3.83 us  [the longest x1 3.82 us: local(): lax.ppermute(going_down, 'col', [(d, (d - 1) % ways) for d in range(ways)])]
  transfers between devices with their start and end apart: 7 -> 9, of which waited for: 7 -> 8; matrix products, arithmetic and copies ran while one was open for 3% -> 4% of each run, Pallas kernels for 0% -> 0%
where the time goes in v1:
time: 210 us; the launch traced here: 209 us
  waiting for transfers between devices  173 us (82%)
  between operations  14.2 us (7%)
  matrix products  13.9 us (7%)
  starting transfers between devices  4.07 us (2%)
  local copies, waits for them, and re-layouts  3.67 us (2%)
    psum x1, waiting for transfers between devices, local(): summed = lax.psum(partial_sums.astype(jnp.bfloat16), 'col')  50 us
    all_gather x1, waiting for transfers between devices, local(): w_rows = lax.all_gather(weight, 'row', axis=1, tiled=True)  26.9 us
    reduce_scatter x1, waiting for transfers between devices, local(): lax.psum_scatter(jnp.dot(programs, w_rows, preferred_element_type=jnp.flo...  26.5 us
    reduce_scatter x1, waiting for transfers between devices, local(): lax.psum_scatter(weight_part.astype(jnp.bfloat16), 'row', scatter_dimensi...  26.5 us
    reduce_scatter x1, waiting for transfers between devices, local(): lax.psum_scatter(test_part.astype(jnp.bfloat16), 'row', scatter_dimension...  25.8 us
    ppermute x2, waiting for transfers between devices, local(): lax.ppermute(going_up, 'col', [(d, (d + 1) % ways) for d in range(ways)])  13.7 us
    dot_general x4, matrix products, contract(): lax.dot_general(left, right, (((left_dim,), (right_dim,)), ((), ())), pre...  9.22 us
  transfers between devices with their start and end apart: 9, of which 8 were waited for; matrix products, arithmetic and copies ran while one was open for 4% of the time, Pallas kernels for 0%

profile of v1, /device:TPU:0, one launch (start us, length us, event | category | flops | bytes accessed | tf_op | source)
XLA Modules:
  0.0 209.2 jit_solution(9522128603655399423)
XLA Ops:
  7.2 0.7 all-gather.3.cloned.1.call-update
  8.0 26.9 %all-gather.3.cloned.1.call-done = bf16[512,2048]{1,0:T(8,128)(2,1)} async-done(((bf16[512,512]{1,0:T(8,128)(2,1)}), bf16[512,2048]{1,0:T(8,128)(2,1)}) %all-gather.3.cloned.1.call-update) | async-done | bytes 2097168 | tf_op jit(solution)/shard_map/all_gather | solution.py:19
  34.9 3.3 %convolution_convert_fusion = bf16[256,2048]{1,0:T(8,128)(2,1)} fusion(bf16[256,512]{1,0:T(8,128)(2,1)S(1)} %copy-done, bf16[512,2048]{1,0:T(8,128)(2,1)} %all-gather.3.cloned.1.call-done), kind=kOutput, calls=%fused_computation.3 | convolution fusion | flops 537395200 | bytes 3407872 | tf_op jit(solution)/shard_map/dot_general | solution.py:21
  38.2 0.0 all-gather.5.cloned.1.call-start
  38.2 0.7 all-gather.5.cloned.1.call-update
  39.0 26.5 %reduce-scatter.4.cloned.1.call-done = bf16[64,2048]{1,0:T(8,128)(2,1)} async-done(((bf16[256,2048]{1,0:T(8,128)(2,1)}), bf16[64,2048]{1,0:T(8,128)(2,1)}) %reduce-scatter.4.cloned.1.call-update) | async-done | bytes 262160 | tf_op jit(solution)/shard_map/reduce_scatter | solution.py:20
  65.5 3.8 %collective-permute-start.1 = (bf16[64,2048]{1,0:T(8,128)(2,1)}, bf16[64,2048]{1,0:T(8,128)(2,1)S(1)}, u32[]{:S(2)}, u32[]{:S(2)}) collective-permute-start(bf16[64,2048]{1,0:T(8,128)(2,1)} %reduce-scatter.4.cloned.1.call-done), channel_id=1, source_target_pairs={{0,3},{1,0},{2,1},{3,2},{4,7},{5,4},{6,5},{7,6},{8,11},{9,8},{10,9... | collective-permute-start | bytes 786440 | tf_op jit(solution)/shard_map/ppermute | solution.py:38
  69.3 0.1 broadcast_in_dim.3
  69.4 1.0 constant_dynamic-update-slice_fusion.3
  70.4 6.3 %collective-permute-done = bf16[64,2048]{1,0:T(8,128)(2,1)S(1)} collective-permute-done((bf16[64,2048]{1,0:T(8,128)(2,1)}, bf16[64,2048]{1,0:T(8,128)(2,1)S(1)}, u32[]{:S(2)}, u32[]{:S(2)}) %collective-permute-start) | collective-permute-done | bytes 262176 | tf_op jit(solution)/shard_map/ppermute | solution.py:33
  76.7 2.5 %collective-permute-done.1 = bf16[64,2048]{1,0:T(8,128)(2,1)S(1)} collective-permute-done((bf16[64,2048]{1,0:T(8,128)(2,1)}, bf16[64,2048]{1,0:T(8,128)(2,1)S(1)}, u32[]{:S(2)}, u32[]{:S(2)}) %collective-permute-start.1) | collective-permute-done | bytes 262176 | tf_op jit(solution)/shard_map/ppermute | solution.py:38
  79.2 7.4 %collective-permute-done.2 = bf16[64,2048]{1,0:T(8,128)(2,1)S(1)} collective-permute-done((bf16[64,2048]{1,0:T(8,128)(2,1)S(1)}, bf16[64,2048]{1,0:T(8,128)(2,1)S(1)}, u32[]{:S(2)}, u32[]{:S(2)}) %collective-permute-start.2) | collective-permute-done | bytes 262176 | tf_op jit(solution)/shard_map/ppermute | solution.py:33
  86.8 1.8 fusion.8
  88.6 1.4 convolution_convert_fusion.1
  90.0 0.0 reduce-scatter.8.cloned.1.call-start
  90.1 50.0 %all-reduce.2.cloned.1.call-done = bf16[256,2048]{1,0:T(8,128)(2,1)} async-done(((bf16[256,2048]{1,0:T(8,128)(2,1)}), bf16[256,2048]{1,0:T(8,128)(2,1)}) %all-reduce.2.cloned.1.call-update) | async-done | bytes 1048592 | tf_op jit(solution)/shard_map/psum | solution.py:46
  140.1 3.3 %fusion = bf16[512,2048]{0,1:T(8,128)(2,1)} fusion(bf16[256,2048]{1,0:T(8,128)(2,1)} %all-reduce.2.cloned.1.call-done, bf16[256,512]{1,0:T(8,128)(2,1)S(1)} %copy-done), kind=kOutput, calls=%fused_computation.1 | convolution fusion | flops 538968064 | bytes 3407872 | tf_op jit(solution)/shard_map/dot_general | solution.py:11
  143.4 0.0 reduce-scatter.6.cloned.1.call-start
  143.5 1.5 fusion.1
  145.0 0.3 copy-done.1
  145.2 2.7 %fusion.2 = bf16[256,512]{1,0:T(8,128)(2,1)} fusion(bf16[256,2048]{1,0:T(8,128)(2,1)} %all-reduce.2.cloned.1.call-done, bf16[512,2048]{1,0:T(8,128)(2,1)S(1)} %copy-done.1), kind=kOutput, calls=%fused_computation.7 | convolution fusion | flops 537133056 | bytes 3407872 | tf_op jit(solution)/shard_map/dot_general | solution.py:11
  147.9 26.5 %reduce-scatter.8.cloned.1.call-done = bf16[512,512]{0,1:T(8,128)(2,1)} async-done(((bf16[512,2048]{0,1:T(8,128)(2,1)}), bf16[512,512]{0,1:T(8,128)(2,1)}) %reduce-scatter.8.cloned.1.call-update) | async-done | bytes 524304 | tf_op jit(solution)/shard_map/reduce_scatter | solution.py:51
  174.4 2.2 %copy.7 = f32[512,512]{1,0:T(8,128)} copy(bf16[512,512]{0,1:T(8,128)(2,1)} %reduce-scatter.8.cloned.1.call-done) | data formatting | bytes 1572864
  176.6 25.8 %reduce-scatter.6.cloned.1.call-done = bf16[256,512]{1,0:T(8,128)(2,1)} async-done(((bf16[256,2048]{1,0:T(8,128)(2,1)}), bf16[256,512]{1,0:T(8,128)(2,1)}) %reduce-scatter.6.cloned.1.call-update) | async-done | bytes 262160 | tf_op jit(solution)/shard_map/reduce_scatter | solution.py:54
  (20 shorter events, 0.3 us)
Async XLA Ops:
  7.2 27.7 %copy-start = (bf16[256,512]{1,0:T(8,128)(2,1)S(1)}, bf16[256,512]{1,0:T(8,128)(2,1)}, u32[]{:S(2)}) copy-start(bf16[256,512]{1,0:T(8,128)(2,1)} %param.4) | copy-start | bytes 786436
  7.2 27.7 %all-gather.3.cloned.1.call-start = ((), (), s32[]{:S(2)}) async-start(), calls=%async_computation.3 | async-start | bytes 2621440 | tf_op jit(solution)/shard_map/all_gather | solution.py:19
  7.9 57.6 %reduce-scatter.4.cloned.1.call-start = ((), (), s32[]{:S(2)}) async-start(), calls=%async_computation.4 | async-start | bytes 1310720 | tf_op jit(solution)/shard_map/reduce_scatter | solution.py:20
  38.2 48.6 %copy-start.3 = (s32[256,256]{1,0:T(8,128)S(1)}, s32[256,256]{1,0:T(8,128)}, u32[]{:S(2)}) copy-start(s32[256,256]{1,0:T(8,128)} %param.7) | copy-start | bytes 786436
  38.2 48.5 %all-gather.5.cloned.1.call-start = ((), (), s32[]{:S(2)}) async-start(), calls=%async_computation.5 | async-start | bytes 1310720 | tf_op jit(solution)/shard_map/all_gather | solution.py:42
  38.9 101.2 %all-reduce.2.cloned.1.call-start = ((), (), s32[]{:S(2)}) async-start(), calls=%async_computation.6 | async-start | bytes 2097152 | tf_op jit(solution)/shard_map/psum | solution.py:46
  65.5 11.2 %collective-permute-start = (bf16[64,2048]{1,0:T(8,128)(2,1)}, bf16[64,2048]{1,0:T(8,128)(2,1)S(1)}, u32[]{:S(2)}, u32[]{:S(2)}) collective-permute-start(bf16[64,2048]{1,0:T(8,128)(2,1)} %reduce-scatter.4.cloned.1.call-done), channel_id=1, source_target_pairs={{0,1},{1,2},{2,3},{3,0},{4,5},{5,6},{6,7},{7,4},{8,9},{9,10},{10,1... | collective-permute-start | bytes 786440 | tf_op jit(solution)/shard_map/ppermute | solution.py:33
  65.5 13.7 %collective-permute-start.1 = (bf16[64,2048]{1,0:T(8,128)(2,1)}, bf16[64,2048]{1,0:T(8,128)(2,1)S(1)}, u32[]{:S(2)}, u32[]{:S(2)}) collective-permute-start(bf16[64,2048]{1,0:T(8,128)(2,1)} %reduce-scatter.4.cloned.1.call-done), channel_id=1, source_target_pairs={{0,3},{1,0},{2,1},{3,2},{4,7},{5,4},{6,5},{7,6},{8,11},{9,8},{10,9... | collective-permute-start | bytes 786440 | tf_op jit(solution)/shard_map/ppermute | solution.py:38
  76.7 10.0 %collective-permute-start.2 = (bf16[64,2048]{1,0:T(8,128)(2,1)S(1)}, bf16[64,2048]{1,0:T(8,128)(2,1)S(1)}, u32[]{:S(2)}, u32[]{:S(2)}) collective-permute-start(bf16[64,2048]{1,0:T(8,128)(2,1)S(1)} %collective-permute-done), channel_id=1, source_target_pairs={{0,1},{1,2},{2,3},{3,0},{4,5},{5,6},{6,7},{7,4},{8,9},{9,10},{10,1... | collective-permute-start | bytes 786440 | tf_op jit(solution)/shard_map/ppermute | solution.py:33
  86.7 1.8 copy-start.2
  90.0 84.4 %reduce-scatter.8.cloned.1.call-start = ((), (), s32[]{:S(2)}) async-start(), calls=%async_computation.8 | async-start | bytes 2621440 | tf_op jit(solution)/shard_map/reduce_scatter | solution.py:51
  143.4 1.8 copy-start.1
  143.4 59.0 %reduce-scatter.6.cloned.1.call-start = ((), (), s32[]{:S(2)}) async-start(), calls=%async_computation.7 | async-start | bytes 1310720 | tf_op jit(solution)/shard_map/reduce_scatter | solution.py:54
Sparse Core Ops, SparseCore 0:
  9.6 25.2 all-gather.2
  38.3 27.1 reduce-scatter.3
  67.1 15.3 all-gather.4
  90.1 49.9 all-reduce.1
  143.5 30.7 reduce-scatter.7
  177.5 24.8 reduce-scatter.5
